TPU v7x, 256 devices: a whole 4x4x8 slice. The times are simulated.
256 devices in a mesh: row: 8 (over x, core), col: 16 (over z, y_hi), layer: 2 (over y_lo).
Axes of the slice: x: 4, y: 4 (y_hi: 2, y_lo: 2; y = y_hi * 2 + y_lo), z: 8, core: 2. Of those that a mesh axis runs over, the one named last changes fastest.
Arguments:
- interface_panel: float32 [2048, 1024], P('col', 'row'), may hold values from -6 to 6
- coupling: float32 [2, 2, 2048, 2048], P('layer', None, 'row', 'col'), may hold values from -0.0625 to 0.0625
- solved_coupling: float32 [8192, 1024], P(('layer', 'col'), 'row'), may hold values from -6 to 6
Outputs:
- schur_panel: float32 [2048, 1024], P('col', 'row')
All inputs are finite; a program needn't handle non-finite values.
Results may differ from a plain program's by a relative error of at most 0.00007.
Values sent between devices are 32-bit elements; how exact they have to be, the bound alone decides.
A program may use at most 64 MiB of HBM per device.

v0:
```python
import jax
import jax.numpy as jnp
from jax import lax
from jax.sharding import PartitionSpec as P


def from_behind(value, axis, steps):
    count = lax.axis_size(axis)
    pairs = [(source, (source + steps) % count) for source in range(count)]
    return lax.ppermute(value, axis, pairs)


def multiply(block, solved):
    return lax.dot_general(
        block,
        solved,
        (((0,), (0,)), ((), ())),
        precision=lax.Precision.HIGHEST,
        preferred_element_type=jnp.float32,
    )


def shards(interface_panel, coupling, solved_coupling):
    blocks = coupling[0]
    rows_here = lax.axis_size("row")
    cols_here = lax.axis_size("col")
    empty = jnp.zeros((blocks.shape[2], solved_coupling.shape[1]), jnp.float32)
    row_id = lax.axis_index("row")
    col_id = lax.axis_index("col")
    for bit in range(cols_here.bit_length() - 1):
        span = 1 << bit
        if span < rows_here:
            moved = from_behind(blocks, "row", -span)
            moved = jnp.where(row_id >= rows_here - span, jnp.roll(moved, -1, axis=0), moved)
        else:
            moved = jnp.roll(blocks, -(span // rows_here), axis=0)
        blocks = jnp.where(col_id // span % 2 == 1, moved, blocks)
    solved = solved_coupling
    for bit in range(rows_here.bit_length() - 1):
        span = 1 << bit
        moved_rows = from_behind(solved, "col", -span)
        solved = jnp.where(row_id // span % 2 == 1, moved_rows, solved)

    def advance(step, carry):
        total, held, current = carry
        total = total + multiply(held[0], current)
        arrived = from_behind(held, "row", -1)
        held = jnp.where(row_id == rows_here - 1, jnp.roll(arrived, -1, axis=0), arrived)
        current = from_behind(current, "col", -1)
        return (total, held, current)

    total, blocks, solved = lax.fori_loop(0, cols_here - 1, advance, (empty, blocks, solved))
    total = total + multiply(blocks[0], solved)
    summed = lax.psum(total, "layer")
    return interface_panel - summed


def solution(mesh):
    return jax.shard_map(
        shards,
        mesh=mesh,
        in_specs=(P("col", "row"), P("layer", None, "row", "col"), P(("layer", "col"), "row")),
        out_specs=P("col", "row"),
        check_vma=False,
    )
```

profile of v0, /device:TPU:2, one launch (start us, length us, event | category | flops | bytes accessed | tf_op | source)
XLA Modules:
  0.0 221.0 jit_solution(10754916581383315818)
XLA Ops:
  6.5 8.5 %collective-permute-start.5 = (f32[256,128]{1,0:T(8,128)}, f32[256,128]{1,0:T(8,128)S(1)}, u32[]{:S(2)}, u32[]{:S(2)}) collective-permute-start(f32[256,128]{1,0:T(8,128)} %param.7), channel_id=1, source_target_pairs={{0,30},{2,0},{4,2},{6,4},{8,6},{10,8},{12,10},{14,12},{16,14},{18,... | collective-permute-start | bytes 393224 | tf_op jit(solution)/shard_map/ppermute | solution.py:10
  15.0 3.1 %collective-permute-done.5 = f32[256,128]{1,0:T(8,128)S(1)} collective-permute-done((f32[256,128]{1,0:T(8,128)}, f32[256,128]{1,0:T(8,128)S(1)}, u32[]{:S(2)}, u32[]{:S(2)}) %collective-permute-start.5) | collective-permute-done | bytes 131104 | tf_op jit(solution)/shard_map/ppermute | solution.py:10
  25.9 3.4 %collective-permute-done.3 = f32[2,256,128]{2,1,0:T(8,128)S(1)} collective-permute-done((f32[2,256,128]{2,1,0:T(8,128)S(1)}, f32[2,256,128]{2,1,0:T(8,128)S(1)}, u32[]{:S(2)}, u32[]{:S(2)}) %collective-permute-start.3) | collective-permute-done | bytes 262176 | tf_op jit(solution)/shard_map/ppermute | solution.py:10
  29.4 3.5 %collective-permute-start.4 = (f32[2,256,128]{2,1,0:T(8,128)S(1)}, f32[2,256,128]{2,1,0:T(8,128)S(1)}, u32[]{:S(2)}, u32[]{:S(2)}) collective-permute-start(f32[2,256,128]{2,1,0:T(8,128)S(1)} %fusion.3), channel_id=1, source_target_pairs={{0,128},{32,160},{64,192},{96,224},{128,0},{160,32},{192,64},{224,... | collective-permute-start | bytes 786440 | tf_op jit(solution)/shard_map/ppermute | solution.py:10
  32.8 6.7 %collective-permute-done.4 = f32[2,256,128]{2,1,0:T(8,128)S(1)} collective-permute-done((f32[2,256,128]{2,1,0:T(8,128)S(1)}, f32[2,256,128]{2,1,0:T(8,128)S(1)}, u32[]{:S(2)}, u32[]{:S(2)}) %collective-permute-start.4) | collective-permute-done | bytes 262176 | tf_op jit(solution)/shard_map/ppermute | solution.py:10
  39.6 139.2 %while.17 = (s32[]{:T(128)}, f32[128,128]{1,0:T(8,128)S(1)}, f32[2,256,128]{2,1,0:T(8,128)S(1)}, f32[256,128]{1,0:T(8,128)S(1)}, pred[]{:T(512)}, /*index=5*/s32[]{:T(128)}, s32[]{:T(128)}) while((s32[]{:T(128)}, f32[128,128]{1,0:T(8,128)S(1)}, f32[2,256,128]{2,1,0:T(8,128)S(1)}, f32[256,128]{1,0:T(8,128)S(1)}, pred[]{:T(512)}, ...), condition=%wide.region_1.2_spmd.clone, body=%wide.region_0.1_spmd.clone.sunk | while | flops 50495488 | bytes 3539120 | solution.py:52
  44.0 3.2 %collective-permute-done.1 = f32[256,128]{1,0:T(8,128)S(1)} collective-permute-done((f32[256,128]{1,0:T(8,128)S(1)}, f32[256,128]{1,0:T(8,128)S(1)}, u32[]{:S(2)}, u32[]{:S(2)}) %collective-permute-start.1) | collective-permute-done | bytes 131104 | tf_op jit(solution)/shard_map/while/body/eval_jaxpr/ppermute | solution.py:10
  47.2 3.2 %collective-permute-start.1 = (f32[256,128]{1,0:T(8,128)S(1)}, f32[256,128]{1,0:T(8,128)S(1)}, u32[]{:S(2)}, u32[]{:S(2)}) collective-permute-start(f32[256,128]{1,0:T(8,128)S(1)} %copy.11), channel_id=1, source_target_pairs={{0,30},{2,0},{4,2},{6,4},{8,6},{10,8},{12,10},{14,12},{16,14},{18,... | collective-permute-start | bytes 393224 | tf_op jit(solution)/shard_map/while/body/eval_jaxpr/ppermute | solution.py:10
  51.1 3.6 %collective-permute-done.1 = f32[256,128]{1,0:T(8,128)S(1)} collective-permute-done((f32[256,128]{1,0:T(8,128)S(1)}, f32[256,128]{1,0:T(8,128)S(1)}, u32[]{:S(2)}, u32[]{:S(2)}) %collective-permute-start.1) | collective-permute-done | bytes 131104 | tf_op jit(solution)/shard_map/while/body/eval_jaxpr/ppermute | solution.py:10
  55.2 4.8 %collective-permute-start.1 = (f32[256,128]{1,0:T(8,128)S(1)}, f32[256,128]{1,0:T(8,128)S(1)}, u32[]{:S(2)}, u32[]{:S(2)}) collective-permute-start(f32[256,128]{1,0:T(8,128)S(1)} %copy.11), channel_id=1, source_target_pairs={{0,30},{2,0},{4,2},{6,4},{8,6},{10,8},{12,10},{14,12},{16,14},{18,... | collective-permute-start | bytes 393224 | tf_op jit(solution)/shard_map/while/body/eval_jaxpr/ppermute | solution.py:10
  60.5 2.9 %collective-permute-done.1 = f32[256,128]{1,0:T(8,128)S(1)} collective-permute-done((f32[256,128]{1,0:T(8,128)S(1)}, f32[256,128]{1,0:T(8,128)S(1)}, u32[]{:S(2)}, u32[]{:S(2)}) %collective-permute-start.1) | collective-permute-done | bytes 131104 | tf_op jit(solution)/shard_map/while/body/eval_jaxpr/ppermute | solution.py:10
  64.7 5.8 %collective-permute-start.1 = (f32[256,128]{1,0:T(8,128)S(1)}, f32[256,128]{1,0:T(8,128)S(1)}, u32[]{:S(2)}, u32[]{:S(2)}) collective-permute-start(f32[256,128]{1,0:T(8,128)S(1)} %copy.11), channel_id=1, source_target_pairs={{0,30},{2,0},{4,2},{6,4},{8,6},{10,8},{12,10},{14,12},{16,14},{18,... | collective-permute-start | bytes 393224 | tf_op jit(solution)/shard_map/while/body/eval_jaxpr/ppermute | solution.py:10
  74.3 5.8 %collective-permute-start.1 = (f32[256,128]{1,0:T(8,128)S(1)}, f32[256,128]{1,0:T(8,128)S(1)}, u32[]{:S(2)}, u32[]{:S(2)}) collective-permute-start(f32[256,128]{1,0:T(8,128)S(1)} %copy.11), channel_id=1, source_target_pairs={{0,30},{2,0},{4,2},{6,4},{8,6},{10,8},{12,10},{14,12},{16,14},{18,... | collective-permute-start | bytes 393224 | tf_op jit(solution)/shard_map/while/body/eval_jaxpr/ppermute | solution.py:10
  83.9 5.8 %collective-permute-start.1 = (f32[256,128]{1,0:T(8,128)S(1)}, f32[256,128]{1,0:T(8,128)S(1)}, u32[]{:S(2)}, u32[]{:S(2)}) collective-permute-start(f32[256,128]{1,0:T(8,128)S(1)} %copy.11), channel_id=1, source_target_pairs={{0,30},{2,0},{4,2},{6,4},{8,6},{10,8},{12,10},{14,12},{16,14},{18,... | collective-permute-start | bytes 393224 | tf_op jit(solution)/shard_map/while/body/eval_jaxpr/ppermute | solution.py:10
  93.5 5.8 %collective-permute-start.1 = (f32[256,128]{1,0:T(8,128)S(1)}, f32[256,128]{1,0:T(8,128)S(1)}, u32[]{:S(2)}, u32[]{:S(2)}) collective-permute-start(f32[256,128]{1,0:T(8,128)S(1)} %copy.11), channel_id=1, source_target_pairs={{0,30},{2,0},{4,2},{6,4},{8,6},{10,8},{12,10},{14,12},{16,14},{18,... | collective-permute-start | bytes 393224 | tf_op jit(solution)/shard_map/while/body/eval_jaxpr/ppermute | solution.py:10
  103.1 5.8 %collective-permute-start.1 = (f32[256,128]{1,0:T(8,128)S(1)}, f32[256,128]{1,0:T(8,128)S(1)}, u32[]{:S(2)}, u32[]{:S(2)}) collective-permute-start(f32[256,128]{1,0:T(8,128)S(1)} %copy.11), channel_id=1, source_target_pairs={{0,30},{2,0},{4,2},{6,4},{8,6},{10,8},{12,10},{14,12},{16,14},{18,... | collective-permute-start | bytes 393224 | tf_op jit(solution)/shard_map/while/body/eval_jaxpr/ppermute | solution.py:10
  112.8 5.8 %collective-permute-start.1 = (f32[256,128]{1,0:T(8,128)S(1)}, f32[256,128]{1,0:T(8,128)S(1)}, u32[]{:S(2)}, u32[]{:S(2)}) collective-permute-start(f32[256,128]{1,0:T(8,128)S(1)} %copy.11), channel_id=1, source_target_pairs={{0,30},{2,0},{4,2},{6,4},{8,6},{10,8},{12,10},{14,12},{16,14},{18,... | collective-permute-start | bytes 393224 | tf_op jit(solution)/shard_map/while/body/eval_jaxpr/ppermute | solution.py:10
  122.4 5.8 %collective-permute-start.1 = (f32[256,128]{1,0:T(8,128)S(1)}, f32[256,128]{1,0:T(8,128)S(1)}, u32[]{:S(2)}, u32[]{:S(2)}) collective-permute-start(f32[256,128]{1,0:T(8,128)S(1)} %copy.11), channel_id=1, source_target_pairs={{0,30},{2,0},{4,2},{6,4},{8,6},{10,8},{12,10},{14,12},{16,14},{18,... | collective-permute-start | bytes 393224 | tf_op jit(solution)/shard_map/while/body/eval_jaxpr/ppermute | solution.py:10
  132.0 5.8 %collective-permute-start.1 = (f32[256,128]{1,0:T(8,128)S(1)}, f32[256,128]{1,0:T(8,128)S(1)}, u32[]{:S(2)}, u32[]{:S(2)}) collective-permute-start(f32[256,128]{1,0:T(8,128)S(1)} %copy.11), channel_id=1, source_target_pairs={{0,30},{2,0},{4,2},{6,4},{8,6},{10,8},{12,10},{14,12},{16,14},{18,... | collective-permute-start | bytes 393224 | tf_op jit(solution)/shard_map/while/body/eval_jaxpr/ppermute | solution.py:10
  141.6 5.8 %collective-permute-start.1 = (f32[256,128]{1,0:T(8,128)S(1)}, f32[256,128]{1,0:T(8,128)S(1)}, u32[]{:S(2)}, u32[]{:S(2)}) collective-permute-start(f32[256,128]{1,0:T(8,128)S(1)} %copy.11), channel_id=1, source_target_pairs={{0,30},{2,0},{4,2},{6,4},{8,6},{10,8},{12,10},{14,12},{16,14},{18,... | collective-permute-start | bytes 393224 | tf_op jit(solution)/shard_map/while/body/eval_jaxpr/ppermute | solution.py:10
  151.2 5.8 %collective-permute-start.1 = (f32[256,128]{1,0:T(8,128)S(1)}, f32[256,128]{1,0:T(8,128)S(1)}, u32[]{:S(2)}, u32[]{:S(2)}) collective-permute-start(f32[256,128]{1,0:T(8,128)S(1)} %copy.11), channel_id=1, source_target_pairs={{0,30},{2,0},{4,2},{6,4},{8,6},{10,8},{12,10},{14,12},{16,14},{18,... | collective-permute-start | bytes 393224 | tf_op jit(solution)/shard_map/while/body/eval_jaxpr/ppermute | solution.py:10
  160.8 5.8 %collective-permute-start.1 = (f32[256,128]{1,0:T(8,128)S(1)}, f32[256,128]{1,0:T(8,128)S(1)}, u32[]{:S(2)}, u32[]{:S(2)}) collective-permute-start(f32[256,128]{1,0:T(8,128)S(1)} %copy.11), channel_id=1, source_target_pairs={{0,30},{2,0},{4,2},{6,4},{8,6},{10,8},{12,10},{14,12},{16,14},{18,... | collective-permute-start | bytes 393224 | tf_op jit(solution)/shard_map/while/body/eval_jaxpr/ppermute | solution.py:10
  170.5 5.8 %collective-permute-start.1 = (f32[256,128]{1,0:T(8,128)S(1)}, f32[256,128]{1,0:T(8,128)S(1)}, u32[]{:S(2)}, u32[]{:S(2)}) collective-permute-start(f32[256,128]{1,0:T(8,128)S(1)} %copy.11), channel_id=1, source_target_pairs={{0,30},{2,0},{4,2},{6,4},{8,6},{10,8},{12,10},{14,12},{16,14},{18,... | collective-permute-start | bytes 393224 | tf_op jit(solution)/shard_map/while/body/eval_jaxpr/ppermute | solution.py:10
  179.9 32.8 %all-reduce.2.cloned.1.call-done = f32[128,128]{1,0:T(8,128)} async-done(((f32[128,128]{1,0:T(8,128)}), f32[128,128]{1,0:T(8,128)}) %all-reduce.2.cloned.1.call-update) | async-done | bytes 65552 | tf_op jit(solution)/shard_map/psum | solution.py:54
  (131 shorter events, 61.4 us)
Async XLA Ops:
  6.5 206.2 %all-reduce.2.cloned.1.call-start = ((), (), s32[]{:S(2)}) async-start(), calls=%async_computation | async-start | bytes 131072 | tf_op jit(solution)/shard_map/psum | solution.py:54
  6.5 11.6 %collective-permute-start.5 = (f32[256,128]{1,0:T(8,128)}, f32[256,128]{1,0:T(8,128)S(1)}, u32[]{:S(2)}, u32[]{:S(2)}) collective-permute-start(f32[256,128]{1,0:T(8,128)} %param.7), channel_id=1, source_target_pairs={{0,30},{2,0},{4,2},{6,4},{8,6},{10,8},{12,10},{14,12},{16,14},{18,... | collective-permute-start | bytes 393224 | tf_op jit(solution)/shard_map/ppermute | solution.py:10
  20.5 8.8 %collective-permute-start.3 = (f32[2,256,128]{2,1,0:T(8,128)S(1)}, f32[2,256,128]{2,1,0:T(8,128)S(1)}, u32[]{:S(2)}, u32[]{:S(2)}) collective-permute-start(f32[2,256,128]{2,1,0:T(8,128)S(1)} %fusion.2), channel_id=1, source_target_pairs={{0,192},{32,224},{64,0},{96,32},{128,64},{160,96},{192,128},{224,1... | collective-permute-start | bytes 786440 | tf_op jit(solution)/shard_map/ppermute | solution.py:10
  24.1 8.7 %collective-permute-start.7 = (f32[256,128]{1,0:T(8,128)S(1)}, f32[256,128]{1,0:T(8,128)S(1)}, u32[]{:S(2)}, u32[]{:S(2)}) collective-permute-start(f32[256,128]{1,0:T(8,128)S(1)} %broadcast_select_fusion.1), channel_id=1, source_target_pairs={{0,24},{2,26},{4,28},{6,30},{8,0},{10,2},{12,4},{14,6},{16,8},{18,... | collective-permute-start | bytes 393224 | tf_op jit(solution)/shard_map/ppermute | solution.py:10
  29.4 10.1 %collective-permute-start.4 = (f32[2,256,128]{2,1,0:T(8,128)S(1)}, f32[2,256,128]{2,1,0:T(8,128)S(1)}, u32[]{:S(2)}, u32[]{:S(2)}) collective-permute-start(f32[2,256,128]{2,1,0:T(8,128)S(1)} %fusion.3), channel_id=1, source_target_pairs={{0,128},{32,160},{64,192},{96,224},{128,0},{160,32},{192,64},{224,... | collective-permute-start | bytes 786440 | tf_op jit(solution)/shard_map/ppermute | solution.py:10
  55.2 8.2 %collective-permute-start.1 = (f32[256,128]{1,0:T(8,128)S(1)}, f32[256,128]{1,0:T(8,128)S(1)}, u32[]{:S(2)}, u32[]{:S(2)}) collective-permute-start(f32[256,128]{1,0:T(8,128)S(1)} %copy.11), channel_id=1, source_target_pairs={{0,30},{2,0},{4,2},{6,4},{8,6},{10,8},{12,10},{14,12},{16,14},{18,... | collective-permute-start | bytes 393224 | tf_op jit(solution)/shard_map/while/body/eval_jaxpr/ppermute | solution.py:10
  64.7 8.4 %collective-permute-start.1 = (f32[256,128]{1,0:T(8,128)S(1)}, f32[256,128]{1,0:T(8,128)S(1)}, u32[]{:S(2)}, u32[]{:S(2)}) collective-permute-start(f32[256,128]{1,0:T(8,128)S(1)} %copy.11), channel_id=1, source_target_pairs={{0,30},{2,0},{4,2},{6,4},{8,6},{10,8},{12,10},{14,12},{16,14},{18,... | collective-permute-start | bytes 393224 | tf_op jit(solution)/shard_map/while/body/eval_jaxpr/ppermute | solution.py:10
  73.0 7.5 %collective-permute-start = (f32[2,256,128]{2,1,0:T(8,128)S(1)}, f32[2,256,128]{2,1,0:T(8,128)S(1)}, u32[]{:S(2)}, u32[]{:S(2)}) collective-permute-start(f32[2,256,128]{2,1,0:T(8,128)S(1)} %get-tuple-element.153), channel_id=1, source_target_pairs={{0,224},{32,0},{64,32},{96,64},{128,96},{160,128},{192,160},{224,1... | collective-permute-start | bytes 786440 | tf_op jit(solution)/shard_map/while/body/eval_jaxpr/ppermute | solution.py:10
  74.3 8.4 %collective-permute-start.1 = (f32[256,128]{1,0:T(8,128)S(1)}, f32[256,128]{1,0:T(8,128)S(1)}, u32[]{:S(2)}, u32[]{:S(2)}) collective-permute-start(f32[256,128]{1,0:T(8,128)S(1)} %copy.11), channel_id=1, source_target_pairs={{0,30},{2,0},{4,2},{6,4},{8,6},{10,8},{12,10},{14,12},{16,14},{18,... | collective-permute-start | bytes 393224 | tf_op jit(solution)/shard_map/while/body/eval_jaxpr/ppermute | solution.py:10
  83.9 8.4 %collective-permute-start.1 = (f32[256,128]{1,0:T(8,128)S(1)}, f32[256,128]{1,0:T(8,128)S(1)}, u32[]{:S(2)}, u32[]{:S(2)}) collective-permute-start(f32[256,128]{1,0:T(8,128)S(1)} %copy.11), channel_id=1, source_target_pairs={{0,30},{2,0},{4,2},{6,4},{8,6},{10,8},{12,10},{14,12},{16,14},{18,... | collective-permute-start | bytes 393224 | tf_op jit(solution)/shard_map/while/body/eval_jaxpr/ppermute | solution.py:10
  93.5 8.4 %collective-permute-start.1 = (f32[256,128]{1,0:T(8,128)S(1)}, f32[256,128]{1,0:T(8,128)S(1)}, u32[]{:S(2)}, u32[]{:S(2)}) collective-permute-start(f32[256,128]{1,0:T(8,128)S(1)} %copy.11), channel_id=1, source_target_pairs={{0,30},{2,0},{4,2},{6,4},{8,6},{10,8},{12,10},{14,12},{16,14},{18,... | collective-permute-start | bytes 393224 | tf_op jit(solution)/shard_map/while/body/eval_jaxpr/ppermute | solution.py:10
  101.9 7.5 %collective-permute-start = (f32[2,256,128]{2,1,0:T(8,128)S(1)}, f32[2,256,128]{2,1,0:T(8,128)S(1)}, u32[]{:S(2)}, u32[]{:S(2)}) collective-permute-start(f32[2,256,128]{2,1,0:T(8,128)S(1)} %get-tuple-element.153), channel_id=1, source_target_pairs={{0,224},{32,0},{64,32},{96,64},{128,96},{160,128},{192,160},{224,1... | collective-permute-start | bytes 786440 | tf_op jit(solution)/shard_map/while/body/eval_jaxpr/ppermute | solution.py:10
  103.1 8.4 %collective-permute-start.1 = (f32[256,128]{1,0:T(8,128)S(1)}, f32[256,128]{1,0:T(8,128)S(1)}, u32[]{:S(2)}, u32[]{:S(2)}) collective-permute-start(f32[256,128]{1,0:T(8,128)S(1)} %copy.11), channel_id=1, source_target_pairs={{0,30},{2,0},{4,2},{6,4},{8,6},{10,8},{12,10},{14,12},{16,14},{18,... | collective-permute-start | bytes 393224 | tf_op jit(solution)/shard_map/while/body/eval_jaxpr/ppermute | solution.py:10
  111.5 7.5 %collective-permute-start = (f32[2,256,128]{2,1,0:T(8,128)S(1)}, f32[2,256,128]{2,1,0:T(8,128)S(1)}, u32[]{:S(2)}, u32[]{:S(2)}) collective-permute-start(f32[2,256,128]{2,1,0:T(8,128)S(1)} %get-tuple-element.153), channel_id=1, source_target_pairs={{0,224},{32,0},{64,32},{96,64},{128,96},{160,128},{192,160},{224,1... | collective-permute-start | bytes 786440 | tf_op jit(solution)/shard_map/while/body/eval_jaxpr/ppermute | solution.py:10
  112.8 8.4 %collective-permute-start.1 = (f32[256,128]{1,0:T(8,128)S(1)}, f32[256,128]{1,0:T(8,128)S(1)}, u32[]{:S(2)}, u32[]{:S(2)}) collective-permute-start(f32[256,128]{1,0:T(8,128)S(1)} %copy.11), channel_id=1, source_target_pairs={{0,30},{2,0},{4,2},{6,4},{8,6},{10,8},{12,10},{14,12},{16,14},{18,... | collective-permute-start | bytes 393224 | tf_op jit(solution)/shard_map/while/body/eval_jaxpr/ppermute | solution.py:10
  121.1 7.5 %collective-permute-start = (f32[2,256,128]{2,1,0:T(8,128)S(1)}, f32[2,256,128]{2,1,0:T(8,128)S(1)}, u32[]{:S(2)}, u32[]{:S(2)}) collective-permute-start(f32[2,256,128]{2,1,0:T(8,128)S(1)} %get-tuple-element.153), channel_id=1, source_target_pairs={{0,224},{32,0},{64,32},{96,64},{128,96},{160,128},{192,160},{224,1... | collective-permute-start | bytes 786440 | tf_op jit(solution)/shard_map/while/body/eval_jaxpr/ppermute | solution.py:10
  122.4 8.4 %collective-permute-start.1 = (f32[256,128]{1,0:T(8,128)S(1)}, f32[256,128]{1,0:T(8,128)S(1)}, u32[]{:S(2)}, u32[]{:S(2)}) collective-permute-start(f32[256,128]{1,0:T(8,128)S(1)} %copy.11), channel_id=1, source_target_pairs={{0,30},{2,0},{4,2},{6,4},{8,6},{10,8},{12,10},{14,12},{16,14},{18,... | collective-permute-start | bytes 393224 | tf_op jit(solution)/shard_map/while/body/eval_jaxpr/ppermute | solution.py:10
  130.7 7.5 %collective-permute-start = (f32[2,256,128]{2,1,0:T(8,128)S(1)}, f32[2,256,128]{2,1,0:T(8,128)S(1)}, u32[]{:S(2)}, u32[]{:S(2)}) collective-permute-start(f32[2,256,128]{2,1,0:T(8,128)S(1)} %get-tuple-element.153), channel_id=1, source_target_pairs={{0,224},{32,0},{64,32},{96,64},{128,96},{160,128},{192,160},{224,1... | collective-permute-start | bytes 786440 | tf_op jit(solution)/shard_map/while/body/eval_jaxpr/ppermute | solution.py:10
  132.0 8.4 %collective-permute-start.1 = (f32[256,128]{1,0:T(8,128)S(1)}, f32[256,128]{1,0:T(8,128)S(1)}, u32[]{:S(2)}, u32[]{:S(2)}) collective-permute-start(f32[256,128]{1,0:T(8,128)S(1)} %copy.11), channel_id=1, source_target_pairs={{0,30},{2,0},{4,2},{6,4},{8,6},{10,8},{12,10},{14,12},{16,14},{18,... | collective-permute-start | bytes 393224 | tf_op jit(solution)/shard_map/while/body/eval_jaxpr/ppermute | solution.py:10
  140.4 7.5 %collective-permute-start = (f32[2,256,128]{2,1,0:T(8,128)S(1)}, f32[2,256,128]{2,1,0:T(8,128)S(1)}, u32[]{:S(2)}, u32[]{:S(2)}) collective-permute-start(f32[2,256,128]{2,1,0:T(8,128)S(1)} %get-tuple-element.153), channel_id=1, source_target_pairs={{0,224},{32,0},{64,32},{96,64},{128,96},{160,128},{192,160},{224,1... | collective-permute-start | bytes 786440 | tf_op jit(solution)/shard_map/while/body/eval_jaxpr/ppermute | solution.py:10
  141.6 8.4 %collective-permute-start.1 = (f32[256,128]{1,0:T(8,128)S(1)}, f32[256,128]{1,0:T(8,128)S(1)}, u32[]{:S(2)}, u32[]{:S(2)}) collective-permute-start(f32[256,128]{1,0:T(8,128)S(1)} %copy.11), channel_id=1, source_target_pairs={{0,30},{2,0},{4,2},{6,4},{8,6},{10,8},{12,10},{14,12},{16,14},{18,... | collective-permute-start | bytes 393224 | tf_op jit(solution)/shard_map/while/body/eval_jaxpr/ppermute | solution.py:10
  151.2 8.4 %collective-permute-start.1 = (f32[256,128]{1,0:T(8,128)S(1)}, f32[256,128]{1,0:T(8,128)S(1)}, u32[]{:S(2)}, u32[]{:S(2)}) collective-permute-start(f32[256,128]{1,0:T(8,128)S(1)} %copy.11), channel_id=1, source_target_pairs={{0,30},{2,0},{4,2},{6,4},{8,6},{10,8},{12,10},{14,12},{16,14},{18,... | collective-permute-start | bytes 393224 | tf_op jit(solution)/shard_map/while/body/eval_jaxpr/ppermute | solution.py:10
  160.8 8.4 %collective-permute-start.1 = (f32[256,128]{1,0:T(8,128)S(1)}, f32[256,128]{1,0:T(8,128)S(1)}, u32[]{:S(2)}, u32[]{:S(2)}) collective-permute-start(f32[256,128]{1,0:T(8,128)S(1)} %copy.11), channel_id=1, source_target_pairs={{0,30},{2,0},{4,2},{6,4},{8,6},{10,8},{12,10},{14,12},{16,14},{18,... | collective-permute-start | bytes 393224 | tf_op jit(solution)/shard_map/while/body/eval_jaxpr/ppermute | solution.py:10
  170.5 8.4 %collective-permute-start.1 = (f32[256,128]{1,0:T(8,128)S(1)}, f32[256,128]{1,0:T(8,128)S(1)}, u32[]{:S(2)}, u32[]{:S(2)}) collective-permute-start(f32[256,128]{1,0:T(8,128)S(1)} %copy.11), channel_id=1, source_target_pairs={{0,30},{2,0},{4,2},{6,4},{8,6},{10,8},{12,10},{14,12},{16,14},{18,... | collective-permute-start | bytes 393224 | tf_op jit(solution)/shard_map/while/body/eval_jaxpr/ppermute | solution.py:10
  (15 other events, 118.1 us)
Sparse Core Ops, SparseCore 0:
  180.0 32.6 all-reduce.1
where the time goes:
time: 222 us; the launch traced here: 221 us
  starting transfers between devices  111 us (50%)
  waiting for transfers between devices  85.5 us (39%)
  between operations  13.5 us (6%)
  matrix products  6.35 us (3%)
  other arithmetic  3.81 us (2%)
    ppermute x36, starting transfers between devices, from_behind(): return lax.ppermute(value, axis, pairs)  111 us
    ppermute x36, waiting for transfers between devices, from_behind(): return lax.ppermute(value, axis, pairs)  52.6 us
    psum x1, waiting for transfers between devices, shards(): summed = lax.psum(total, 'layer')  32.8 us
    dot_general x16, matrix products, multiply(): lax.dot_general(block, solved, (((0,), (0,)), ((), ())), precision=lax.Pr...  6.35 us
  transfers between devices with their start and end apart: 37, of which 22 were waited for; matrix products, arithmetic and copies ran while one was open for 4% of the time, Pallas kernels for 0%

commit v1 on v0

v1 whole, which is shorter than its diff:
```python
import jax
import jax.numpy as jnp
from jax import lax
from jax.sharding import PartitionSpec as P


def shards(interface_panel, coupling, solved_coupling):
    blocks = coupling[0]
    depth = blocks.shape[0] * blocks.shape[1] * lax.axis_size("row")
    gathered_b = lax.all_gather(blocks, "row", axis=1, tiled=True).reshape(depth, blocks.shape[2])
    gathered_y = lax.all_gather(solved_coupling, "col", axis=0, tiled=True)
    partial = lax.dot_general(
        gathered_b,
        gathered_y,
        (((0,), (0,)), ((), ())),
        precision=lax.Precision.HIGHEST,
        preferred_element_type=jnp.float32,
    )
    other = lax.ppermute(partial, "layer", [(0, 1), (1, 0)])
    return interface_panel - (partial + other)


def solution(mesh):
    return jax.shard_map(
        shards,
        mesh=mesh,
        in_specs=(P("col", "row"), P("layer", None, "row", "col"), P(("layer", "col"), "row")),
        out_specs=P("col", "row"),
        check_vma=False,
    )
```

time: 222 us -> 146 us (0.66)
  starting transfers between devices: 111 us -> 0.71 us
  waiting for transfers between devices: 85.5 us -> 125 us
  other arithmetic: 3.81 us -> 0.64 us
    all_gather x0 -> x2, waiting for transfers between devices: none -> 120 us  [the longest x1 89.4 us: shards(): gathered_y = lax.all_gather(solved_coupling, 'col', axis=0, tiled=True)]
    ppermute x36 -> x1, starting transfers between devices: 111 us -> 0.67 us  [shards(): other = lax.ppermute(partial, 'layer', [(0, 1), (1, 0)])]
    ppermute x36 -> x1, waiting for transfers between devices: 52.6 us -> 3.68 us  [shards(): other = lax.ppermute(partial, 'layer', [(0, 1), (1, 0)])]
    psum x1 -> x0, waiting for transfers between devices: 32.8 us -> none  [shards(): summed = lax.psum(total, 'layer')]
    dot_general x16 -> x1, matrix products: 6.35 us -> 5.7 us  [shards(): lax.dot_general(gathered_b, gathered_y, (((0,), (0,)), ((), ())), precisi...]
  transfers between devices with their start and end apart: 37 -> 3, of which waited for: 22 -> 3; matrix products, arithmetic and copies ran while one was open for 4% -> 0% of each run, Pallas kernels for 0% -> 0%
where the time goes in v1:
time: 146 us
  waiting for transfers between devices  125 us (86%)
  between operations  13.4 us (9%)
  matrix products  5.7 us (4%)
    all_gather x1, waiting for transfers between devices, shards(): gathered_y = lax.all_gather(solved_coupling, 'col', axis=0, tiled=True)  89.4 us
    all_gather x1, waiting for transfers between devices, shards(): lax.all_gather(blocks, 'row', axis=1, tiled=True)  31 us
    dot_general x1, matrix products, shards(): lax.dot_general(gathered_b, gathered_y, (((0,), (0,)), ((), ())), precisi...  5.7 us
    ppermute x1, waiting for transfers between devices, shards(): other = lax.ppermute(partial, 'layer', [(0, 1), (1, 0)])  3.68 us
  transfers between devices with their start and end apart: 3, of which 3 were waited for; matrix products, arithmetic and copies ran while one was open for 0% of the time, Pallas kernels for 0%

profile of v1, /device:TPU:2, one launch (start us, length us, event | category | flops | bytes accessed | tf_op | source)
XLA Modules:
  0.0 145.9 jit_solution(16994233739036828383)
XLA Ops:
  6.5 0.0 all-gather.6.cloned.1.call-start
  6.5 0.7 all-gather.6.cloned.1.call-update
  7.3 0.0 all-gather.4.cloned.1.call-start
  7.3 0.7 all-gather.4.cloned.1.call-update
  8.0 31.0 %all-gather.6.cloned.1.call-done = f32[1,2,2048,128]{3,2,1,0:T(8,128)} async-done(((f32[1,2,256,128]{3,2,1,0:T(8,128)}), f32[1,2,2048,128]{3,2,1,0:T(8,128)}) %all-gather.6.cloned.1.call-update) | async-done | bytes 2097168 | tf_op jit(solution)/shard_map/all_gather | solution.py:10
  39.0 89.4 %all-gather.4.cloned.1.call-done = f32[4096,128]{1,0:T(8,128)} async-done(((f32[256,128]{1,0:T(8,128)}), f32[4096,128]{1,0:T(8,128)}) %all-gather.4.cloned.1.call-update) | async-done | bytes 2097168 | tf_op jit(solution)/shard_map/all_gather | solution.py:11
  128.4 0.0 copy-start
  128.4 5.7 %fusion = f32[128,128]{1,0:T(8,128)S(1)} fusion(f32[4096,128]{1,0:T(8,128)} %bitcast.3, f32[4096,128]{1,0:T(8,128)} %all-gather.4.cloned.1.call-done), kind=kOutput, calls=%fused_computation.1 | convolution fusion | flops 805306368 | bytes 4259840 | tf_op jit(solution)/shard_map/dot_general | solution.py:12
  134.1 0.7 collective-permute-start
  134.7 3.7 %collective-permute-done = f32[128,128]{1,0:T(8,128)S(1)} collective-permute-done((f32[128,128]{1,0:T(8,128)S(1)}, f32[128,128]{1,0:T(8,128)S(1)}, u32[]{:S(2)}, u32[]{:S(2)}) %collective-permute-start) | collective-permute-done | bytes 65568 | tf_op jit(solution)/shard_map/ppermute | solution.py:19
  138.4 0.0 copy-done
  138.4 0.6 add_subtract_fusion
Async XLA Ops:
  6.5 32.4 %all-gather.6.cloned.1.call-start = ((), (), s32[]{:S(2)}) async-start(), calls=%async_computation.1 | async-start | bytes 2359296 | tf_op jit(solution)/shard_map/all_gather | solution.py:10
  7.3 121.1 %all-gather.4.cloned.1.call-start = ((), (), s32[]{:S(2)}) async-start(), calls=%async_computation | async-start | bytes 2228224 | tf_op jit(solution)/shard_map/all_gather | solution.py:11
  128.4 10.1 %copy-start = (f32[128,128]{1,0:T(8,128)S(1)}, f32[128,128]{1,0:T(8,128)}, u32[]{:S(2)}) copy-start(f32[128,128]{1,0:T(8,128)} %param.3) | copy-start | bytes 196612
  134.1 4.4 %collective-permute-start = (f32[128,128]{1,0:T(8,128)S(1)}, f32[128,128]{1,0:T(8,128)S(1)}, u32[]{:S(2)}, u32[]{:S(2)}) collective-permute-start(f32[128,128]{1,0:T(8,128)S(1)} %fusion), channel_id=1, source_target_pairs={{0,1},{1,0},{2,3},{3,2},{4,5},{5,4},{6,7},{7,6},{8,9},{9,8},{10,11... | collective-permute-start | bytes 196616 | tf_op jit(solution)/shard_map/ppermute | solution.py:19
Sparse Core Ops, SparseCore 0:
  9.2 29.7 all-gather.5
  41.6 86.7 all-gather.3

commit v2 on v1

v2 whole, which is shorter than its diff:
```python
import jax
import jax.numpy as jnp
from jax import lax
from jax.experimental import pallas as pl
from jax.experimental.pallas import tpu as pltpu
from jax.sharding import PartitionSpec as P

MESH = pl.DeviceIdType.MESH


def multiply(block, solved):
    return lax.dot_general(
        block,
        solved,
        (((0,), (0,)), ((), ())),
        precision=lax.Precision.HIGHEST,
        preferred_element_type=jnp.float32,
    )


def kernel(a_ref, b_ref, y_ref, o_ref, b_all, y_all, mine, theirs,
           b_send, b_recv, y_send, y_recv, p_send, p_recv):
    n_row = lax.axis_size("row")
    n_col = lax.axis_size("col")
    r = lax.axis_index("row")
    c = lax.axis_index("col")
    l = lax.axis_index("layer")
    partner = 1 - l

    def row_peer(d):
        return ((r + d) % n_row, c, l)

    def col_peer(d):
        return (r, (c + d) % n_col, l)

    barrier = pltpu.get_barrier_semaphore()
    for d in range(1, n_row):
        pl.semaphore_signal(barrier, 1, device_id=row_peer(d), device_id_type=MESH)
    for d in range(1, n_col):
        pl.semaphore_signal(barrier, 1, device_id=col_peer(d), device_id_type=MESH)
    pl.semaphore_signal(barrier, 1, device_id=(r, c, partner), device_id_type=MESH)
    pl.semaphore_wait(barrier, (n_row - 1) + (n_col - 1) + 1)

    sends = []
    for d in range(1, n_row):
        copy = pltpu.make_async_remote_copy(
            b_ref.at[0], b_all.at[r], b_send.at[d], b_recv.at[r],
            device_id=row_peer(d), device_id_type=MESH)
        copy.start()
        sends.append(copy)
    for d in range(1, n_col):
        copy = pltpu.make_async_remote_copy(
            y_ref, y_all.at[c], y_send.at[d], y_recv.at[c],
            device_id=col_peer(d), device_id_type=MESH)
        copy.start()
        sends.append(copy)

    b_all[r] = b_ref[0]
    y_all[c] = y_ref[...]

    for d in range(1, n_row):
        source = (r + n_row - d) % n_row
        pltpu.make_async_remote_copy(
            b_ref.at[0], b_all.at[source], b_send.at[d], b_recv.at[source],
            device_id=row_peer(d), device_id_type=MESH).wait_recv()

    total = jnp.zeros(mine.shape, jnp.float32)
    for d in range(n_col):
        source = (c + n_col - d) % n_col
        if d > 0:
            pltpu.make_async_remote_copy(
                y_ref, y_all.at[source], y_send.at[d], y_recv.at[source],
                device_id=col_peer(d), device_id_type=MESH).wait_recv()
        block = b_all[source % n_row, source // n_row]
        total = total + multiply(block, y_all[source])
    mine[...] = total

    swap = pltpu.make_async_remote_copy(
        mine, theirs, p_send.at[0], p_recv.at[0],
        device_id=(r, c, partner), device_id_type=MESH)
    swap.start()
    swap.wait()
    o_ref[...] = a_ref[...] - (mine[...] + theirs[...])
    for copy in sends:
        copy.wait_send()


def shards(interface_panel, coupling, solved_coupling):
    n_row = lax.axis_size("row")
    n_col = lax.axis_size("col")
    _, slots, depth, width = coupling.shape
    vmem = pl.BlockSpec(memory_space=pltpu.VMEM)
    rows, cols = interface_panel.shape
    return pl.pallas_call(
        kernel,
        out_shape=jax.ShapeDtypeStruct((rows, cols), jnp.float32),
        in_specs=[vmem, vmem, vmem],
        out_specs=vmem,
        scratch_shapes=[
            pltpu.VMEM((n_row, slots, depth, width), jnp.float32),
            pltpu.VMEM((n_col,) + solved_coupling.shape, jnp.float32),
            pltpu.VMEM((rows, cols), jnp.float32),
            pltpu.VMEM((rows, cols), jnp.float32),
            pltpu.SemaphoreType.DMA((n_row,)),
            pltpu.SemaphoreType.DMA((n_row,)),
            pltpu.SemaphoreType.DMA((n_col,)),
            pltpu.SemaphoreType.DMA((n_col,)),
            pltpu.SemaphoreType.DMA((1,)),
            pltpu.SemaphoreType.DMA((1,)),
        ],
        compiler_params=pltpu.CompilerParams(collective_id=0, has_side_effects=True),
    )(interface_panel, coupling, solved_coupling)


def solution(mesh):
    return jax.shard_map(
        shards,
        mesh=mesh,
        in_specs=(P("col", "row"), P("layer", None, "row", "col"), P(("layer", "col"), "row")),
        out_specs=P("col", "row"),
        check_vma=False,
    )
```

time: 146 us -> 66.5 us (0.46)
  the two profiles are of different devices: /device:TPU:2 before, /device:TPU:80 now
where the time goes in v2:
time: 66.5 us; the launch traced here: 66.4 us
  Pallas kernels  64.9 us (98%)
  local copies, waits for them, and re-layouts  1.47 us (2%)
    pallas_call x1, Pallas kernels, shards(): pl.pallas_call(kernel, out_shape=jax.ShapeDtypeStruct((rows, cols), jnp.f...  64.9 us
    unnamed x1, local copies, waits for them, and re-layouts  1.47 us

profile of v2, /device:TPU:80, one launch (start us, length us, event | category | flops | bytes accessed | tf_op | source)
XLA Modules:
  0.0 66.4 jit_solution(7134314343571150009)
XLA Ops:
  0.0 64.9 %shard_map.37 = f32[128,128]{1,0:T(8,128)} custom-call(f32[128,128]{1,0:T(8,128)} %a_ref.1, f32[1,2,256,128]{3,2,1,0:T(8,128)} %b_ref.1, f32[256,128]{1,0:T(8,128)} %y_ref.1), custom_call_target="tpu_custom_call" | custom-call | tf_op jit(solution)/shard_map/pallas_call | solution.py:94
  64.9 1.5 %copy.5 = f32[128,128]{1,0:T(8,128)} copy(f32[128,128]{1,0:T(8,128)} %shard_map.37) | data formatting | bytes 131072

commit v3 on v2

--- a/solution.py
+++ b/solution.py
@@ -22,62 +22,132 @@
            b_send, b_recv, y_send, y_recv, p_send, p_recv):
     n_row = lax.axis_size("row")
     n_col = lax.axis_size("col")
+    n_chip = n_row // 2
+    n_z = n_col // 2
     r = lax.axis_index("row")
     c = lax.axis_index("col")
     l = lax.axis_index("layer")
-    partner = 1 - l
+    chip, core = r // 2, r % 2
+    z, half = c // 2, c % 2
+    other = 1 - half
 
-    def row_peer(d):
-        return ((r + d) % n_row, c, l)
+    def row_dev(row):
+        return (row, c, l)
 
-    def col_peer(d):
-        return (r, (c + d) % n_col, l)
+    def col_dev(col):
+        return (r, col, l)
+
+    def col_of(zz, h):
+        return ((zz + n_z) % n_z) * 2 + h
+
+    cw = col_of(z + 1, half)
+    ccw = col_of(z - 1, half)
+    partner_col = col_of(z, other)
+    on_chip = chip * 2 + (1 - core)
+
+    def far_row(d):
+        return ((chip + d) % n_chip) * 2 + core
 
     barrier = pltpu.get_barrier_semaphore()
-    for d in range(1, n_row):
-        pl.semaphore_signal(barrier, 1, device_id=row_peer(d), device_id_type=MESH)
-    for d in range(1, n_col):
-        pl.semaphore_signal(barrier, 1, device_id=col_peer(d), device_id_type=MESH)
-    pl.semaphore_signal(barrier, 1, device_id=(r, c, partner), device_id_type=MESH)
-    pl.semaphore_wait(barrier, (n_row - 1) + (n_col - 1) + 1)
+    peers = [row_dev(far_row(d)) for d in range(1, n_chip)]
+    peers += [row_dev(on_chip), col_dev(partner_col), col_dev(cw), col_dev(ccw), (r, c, 1 - l)]
+    for peer in peers:
+        pl.semaphore_signal(barrier, 1, device_id=peer, device_id_type=MESH)
+    pl.semaphore_wait(barrier, len(peers))
 
     sends = []
-    for d in range(1, n_row):
+
+    def send(src, dst, sems, recv_sems, slot, device):
         copy = pltpu.make_async_remote_copy(
-            b_ref.at[0], b_all.at[r], b_send.at[d], b_recv.at[r],
-            device_id=row_peer(d), device_id_type=MESH)
-        copy.start()
-        sends.append(copy)
-    for d in range(1, n_col):
-        copy = pltpu.make_async_remote_copy(
-            y_ref, y_all.at[c], y_send.at[d], y_recv.at[c],
-            device_id=col_peer(d), device_id_type=MESH)
+            src, dst.at[slot], sems.at[len(sends)], recv_sems.at[slot],
+            device_id=device, device_id_type=MESH)
         copy.start()
         sends.append(copy)
 
+    def arrival(src, dst, recv_sems, slot):
+        pltpu.make_async_remote_copy(
+            src, dst.at[slot], recv_sems.at[slot], recv_sems.at[slot],
+            device_id=(r, c, 1 - l), device_id_type=MESH).wait_recv()
+
+    for d in range(1, n_chip):
+        send(b_ref.at[0], b_all, b_send, b_recv, r, row_dev(far_row(d)))
+    send(b_ref.at[0], b_all, b_send, b_recv, r, row_dev(on_chip))
+    b_sends = len(sends)
+
+    y_base = len(sends)
+
+    def y_send_slot(src, slot, col):
+        copy = pltpu.make_async_remote_copy(
+            src, y_all.at[slot], y_send.at[len(sends) - y_base], y_recv.at[slot],
+            device_id=col_dev(col), device_id_type=MESH)
+        copy.start()
+        sends.append(copy)
+
+    def y_arrival(slot):
+        arrival(y_ref, y_all, y_recv, slot)
+
+    own_cw, own_ccw = n_z // 2, (n_z - 1) // 2
+    far_cw, far_ccw = (n_z - 1) // 2, n_z // 2
+
+    y_send_slot(y_ref, c, partner_col)
+    if own_cw >= 1:
+        y_send_slot(y_ref, c, cw)
+    if own_ccw >= 1:
+        y_send_slot(y_ref, c, ccw)
     b_all[r] = b_ref[0]
     y_all[c] = y_ref[...]
+    y_arrival(partner_col)
+    if far_cw >= 1:
+        y_send_slot(y_all.at[partner_col], partner_col, cw)
+    if far_ccw >= 1:
+        y_send_slot(y_all.at[partner_col], partner_col, ccw)
+    for t in range(2, n_z // 2 + 1):
+        if t <= own_cw:
+            slot = col_of(z - (t - 1), half)
+            y_arrival(slot)
+            y_send_slot(y_all.at[slot], slot, cw)
+        if t <= own_ccw:
+            slot = col_of(z + (t - 1), half)
+            y_arrival(slot)
+            y_send_slot(y_all.at[slot], slot, ccw)
+        if t <= far_cw:
+            slot = col_of(z - (t - 1), other)
+            y_arrival(slot)
+            y_send_slot(y_all.at[slot], slot, cw)
+        if t <= far_ccw:
+            slot = col_of(z + (t - 1), other)
+            y_arrival(slot)
+            y_send_slot(y_all.at[slot], slot, ccw)
+    if own_cw >= 1:
+        y_arrival(col_of(z - own_cw, half))
+    if own_ccw >= 1:
+        y_arrival(col_of(z + own_ccw, half))
+    if far_cw >= 1:
+        y_arrival(col_of(z - far_cw, other))
+    if far_ccw >= 1:
+        y_arrival(col_of(z + far_ccw, other))
 
-    for d in range(1, n_row):
-        source = (r + n_row - d) % n_row
-        pltpu.make_async_remote_copy(
-            b_ref.at[0], b_all.at[source], b_send.at[d], b_recv.at[source],
-            device_id=row_peer(d), device_id_type=MESH).wait_recv()
+    relay_base = len(sends)
+    for d in range(1, n_chip):
+        slot = far_row(d)
+        arrival(b_ref.at[0], b_all, b_recv, slot)
+        copy = pltpu.make_async_remote_copy(
+            b_all.at[slot], b_all.at[slot], b_send.at[b_sends + len(sends) - relay_base],
+            b_recv.at[slot], device_id=row_dev(on_chip), device_id_type=MESH)
+        copy.start()
+        sends.append(copy)
+    arrival(b_ref.at[0], b_all, b_recv, on_chip)
+    for d in range(1, n_chip):
+        arrival(b_ref.at[0], b_all, b_recv, ((chip + d) % n_chip) * 2 + (1 - core))
 
     total = jnp.zeros(mine.shape, jnp.float32)
-    for d in range(n_col):
-        source = (c + n_col - d) % n_col
-        if d > 0:
-            pltpu.make_async_remote_copy(
-                y_ref, y_all.at[source], y_send.at[d], y_recv.at[source],
-                device_id=col_peer(d), device_id_type=MESH).wait_recv()
-        block = b_all[source % n_row, source // n_row]
-        total = total + multiply(block, y_all[source])
+    for jj in range(n_col):
+        total = total + multiply(b_all[jj % n_row, jj // n_row], y_all[jj])
     mine[...] = total
 
     swap = pltpu.make_async_remote_copy(
         mine, theirs, p_send.at[0], p_recv.at[0],
-        device_id=(r, c, partner), device_id_type=MESH)
+        device_id=(r, c, 1 - l), device_id_type=MESH)
     swap.start()
     swap.wait()
     o_ref[...] = a_ref[...] - (mine[...] + theirs[...])

time: 66.5 us -> 43.1 us (0.65)
  the two profiles are of different devices: /device:TPU:80 before, /device:TPU:1 now
where the time goes in v3:
time: 43.1 us; the launch traced here: 43 us
  Pallas kernels  41.5 us (96%)
  local copies, waits for them, and re-layouts  1.47 us (3%)
    pallas_call x1, Pallas kernels, shards(): pl.pallas_call(kernel, out_shape=jax.ShapeDtypeStruct((rows, cols), jnp.f...  41.5 us
    unnamed x1, local copies, waits for them, and re-layouts  1.47 us

profile of v3, /device:TPU:1, one launch (start us, length us, event | category | flops | bytes accessed | tf_op | source)
XLA Modules:
  0.0 43.0 jit_solution(8718292302876402613)
XLA Ops:
  0.0 41.5 %shard_map.37 = f32[128,128]{1,0:T(8,128)} custom-call(f32[128,128]{1,0:T(8,128)} %a_ref.1, f32[1,2,256,128]{3,2,1,0:T(8,128)} %b_ref.1, f32[256,128]{1,0:T(8,128)} %y_ref.1), custom_call_target="tpu_custom_call" | custom-call | tf_op jit(solution)/shard_map/pallas_call | solution.py:164
  41.5 1.5 %copy.5 = f32[128,128]{1,0:T(8,128)} copy(f32[128,128]{1,0:T(8,128)} %shard_map.37) | data formatting | bytes 131072

commit v4 on v3

v4 whole, which is shorter than its diff:
```python
import jax
import jax.numpy as jnp
from jax import lax
from jax.experimental import pallas as pl
from jax.experimental.pallas import tpu as pltpu
from jax.sharding import PartitionSpec as P

MESH = pl.DeviceIdType.MESH


def multiply(block, solved):
    return lax.dot_general(
        block,
        solved,
        (((0,), (0,)), ((), ())),
        precision=lax.Precision.HIGHEST,
        preferred_element_type=jnp.float32,
    )


def kernel(a_ref, b_ref, y_ref, o_ref, b_all, y_all, own_part, far_part, got_far, summed, got_sum,
           b_send, b_recv, y_send, y_recv, p_send, p_recv):
    n_row = lax.axis_size("row")
    n_col = lax.axis_size("col")
    n_chip = n_row // 2
    n_z = n_col // 2
    slots = b_ref.shape[1]
    r = lax.axis_index("row")
    c = lax.axis_index("col")
    l = lax.axis_index("layer")
    chip, core = r // 2, r % 2
    z, half = c // 2, c % 2
    keeper = core == half

    def col_of(zz, h):
        return ((zz + n_z) % n_z) * 2 + h

    cw = col_of(z + 1, half)
    ccw = col_of(z - 1, half)
    partner_col = col_of(z, 1 - half)
    on_chip = chip * 2 + (1 - core)

    def far_row(d):
        return ((chip + d) % n_chip) * 2 + core

    cross = (on_chip, partner_col, l)
    diagonal = (r, partner_col, 1 - l)
    layer_peer = (r, c, 1 - l)

    barrier = pltpu.get_barrier_semaphore()
    peers = [(far_row(d), c, l) for d in range(1, n_chip)]
    peers += [(on_chip, c, l), cross, (r, cw, l), (r, ccw, l), diagonal, layer_peer]
    for peer in peers:
        pl.semaphore_signal(barrier, 1, device_id=peer, device_id_type=MESH)
    pl.semaphore_wait(barrier, len(peers))

    def arrival(src, dst, recv_sems, slot):
        pltpu.make_async_remote_copy(
            src, dst.at[slot], recv_sems.at[slot], recv_sems.at[slot],
            device_id=layer_peer, device_id_type=MESH).wait_recv()

    local_fill = pltpu.make_async_copy(b_ref.at[0], b_all.at[r], b_recv.at[r])
    cross_fill = pltpu.make_async_remote_copy(
        b_ref.at[0], b_all.at[on_chip], b_send.at[0], b_recv.at[on_chip],
        device_id=cross, device_id_type=MESH)

    @pl.when(keeper)
    def _():
        local_fill.start()

    @pl.when(jnp.logical_not(keeper))
    def _():
        cross_fill.start()

    sends = []

    def y_send_slot(src, slot, col):
        copy = pltpu.make_async_remote_copy(
            src, y_all.at[slot], y_send.at[len(sends)], y_recv.at[slot],
            device_id=(r, col, l), device_id_type=MESH)
        copy.start()
        sends.append(copy)

    def y_arrival(slot):
        arrival(y_ref, y_all, y_recv, slot)

    own_cw, own_ccw = n_z // 2, (n_z - 1) // 2
    if own_cw >= 1:
        y_send_slot(y_ref, c, cw)
    if own_ccw >= 1:
        y_send_slot(y_ref, c, ccw)
    y_all[c] = y_ref[...]

    @pl.when(keeper)
    def _():
        local_fill.wait()

    @pl.when(jnp.logical_not(keeper))
    def _():
        arrival(b_ref.at[0], b_all, b_recv, r)

    b_sends = []

    def b_send_slot(slot, row):
        copy = pltpu.make_async_remote_copy(
            b_all.at[slot], b_all.at[slot], b_send.at[1 + len(b_sends)], b_recv.at[slot],
            device_id=(row, c, l), device_id_type=MESH)
        copy.start()
        b_sends.append(copy)

    for d in range(1, n_chip):
        b_send_slot(r, far_row(d))
    b_send_slot(r, on_chip)

    for t in range(2, n_z // 2 + 1):
        if t <= own_cw:
            slot = col_of(z - (t - 1), half)
            y_arrival(slot)
            y_send_slot(y_all.at[slot], slot, cw)
        if t <= own_ccw:
            slot = col_of(z + (t - 1), half)
            y_arrival(slot)
            y_send_slot(y_all.at[slot], slot, ccw)

    for d in range(1, n_chip):
        slot = far_row(d)
        arrival(b_ref.at[0], b_all, b_recv, slot)
        b_send_slot(slot, on_chip)

    if own_cw >= 1:
        y_arrival(col_of(z - own_cw, half))
    if own_ccw >= 1:
        y_arrival(col_of(z + own_ccw, half))
    arrival(b_ref.at[0], b_all, b_recv, on_chip)
    for d in range(1, n_chip):
        arrival(b_ref.at[0], b_all, b_recv, ((chip + d) % n_chip) * 2 + (1 - core))

    own = jnp.zeros(own_part.shape, jnp.float32)
    far = jnp.zeros(far_part.shape, jnp.float32)
    for s in range(slots):
        for x in range(n_chip):
            jj = s * n_row + 2 * x + half
            solved = y_all[jj]
            own = own + multiply(b_all[2 * x + half, s], solved)
            far = far + multiply(b_all[2 * x + 1 - half, s], solved)
    own_part[...] = own
    far_part[...] = far

    first = pltpu.make_async_remote_copy(
        far_part, got_far, p_send.at[0], p_recv.at[0],
        device_id=diagonal, device_id_type=MESH)
    first.start()
    first.wait()
    summed[...] = own_part[...] + got_far[...]
    second = pltpu.make_async_remote_copy(
        summed, got_sum, p_send.at[1], p_recv.at[1],
        device_id=layer_peer, device_id_type=MESH)
    second.start()
    second.wait()
    o_ref[...] = a_ref[...] - (summed[...] + got_sum[...])

    for copy in sends + b_sends:
        copy.wait_send()

    @pl.when(jnp.logical_not(keeper))
    def _():
        cross_fill.wait_send()


def shards(interface_panel, coupling, solved_coupling):
    n_row = lax.axis_size("row")
    n_col = lax.axis_size("col")
    _, slots, depth, width = coupling.shape
    vmem = pl.BlockSpec(memory_space=pltpu.VMEM)
    rows, cols = interface_panel.shape
    part = pltpu.VMEM((rows, cols), jnp.float32)
    return pl.pallas_call(
        kernel,
        out_shape=jax.ShapeDtypeStruct((rows, cols), jnp.float32),
        in_specs=[vmem, vmem, vmem],
        out_specs=vmem,
        scratch_shapes=[
            pltpu.VMEM((n_row, slots, depth, width), jnp.float32),
            pltpu.VMEM((n_col,) + solved_coupling.shape, jnp.float32),
            part, part, part, part, part,
            pltpu.SemaphoreType.DMA((n_row + 1,)),
            pltpu.SemaphoreType.DMA((n_row,)),
            pltpu.SemaphoreType.DMA((n_col,)),
            pltpu.SemaphoreType.DMA((n_col,)),
            pltpu.SemaphoreType.DMA((2,)),
            pltpu.SemaphoreType.DMA((2,)),
        ],
        compiler_params=pltpu.CompilerParams(collective_id=0, has_side_effects=True),
    )(interface_panel, coupling, solved_coupling)


def solution(mesh):
    return jax.shard_map(
        shards,
        mesh=mesh,
        in_specs=(P("col", "row"), P("layer", None, "row", "col"), P(("layer", "col"), "row")),
        out_specs=P("col", "row"),
        check_vma=False,
    )
```

time: 43.1 us -> 40 us (0.928)
  the two profiles are of different devices: /device:TPU:1 before, /device:TPU:2 now
where the time goes in v4:
time: 40 us; the launch traced here: 39.4 us
  Pallas kernels  37.9 us (95%)
  local copies, waits for them, and re-layouts  1.47 us (4%)
    pallas_call x1, Pallas kernels, shards(): pl.pallas_call(kernel, out_shape=jax.ShapeDtypeStruct((rows, cols), jnp.f...  37.9 us
    unnamed x1, local copies, waits for them, and re-layouts  1.47 us

profile of v4, /device:TPU:2, one launch (start us, length us, event | category | flops | bytes accessed | tf_op | source)
XLA Modules:
  0.0 39.4 jit_solution(7179000236546301403)
XLA Ops:
  0.0 37.9 %shard_map.37 = f32[128,128]{1,0:T(8,128)} custom-call(f32[128,128]{1,0:T(8,128)} %a_ref.1, f32[1,2,256,128]{3,2,1,0:T(8,128)} %b_ref.1, f32[256,128]{1,0:T(8,128)} %y_ref.1), custom_call_target="tpu_custom_call" | custom-call | tf_op jit(solution)/shard_map/pallas_call | solution.py:177
  37.9 1.5 %copy.5 = f32[128,128]{1,0:T(8,128)} copy(f32[128,128]{1,0:T(8,128)} %shard_map.37) | data formatting | bytes 131072

commit v5 on v4

--- a/solution.py
+++ b/solution.py
@@ -18,7 +18,7 @@
     )
 
 
-def kernel(a_ref, b_ref, y_ref, o_ref, b_all, y_all, own_part, far_part, got_far, summed, got_sum,
+def kernel(a_ref, b_ref, y_ref, o_ref, b_all, y_all, own_part, far_part, got_diag, got_plane, got_layer,
            b_send, b_recv, y_send, y_recv, p_send, p_recv):
     n_row = lax.axis_size("row")
     n_col = lax.axis_size("col")
@@ -45,11 +45,12 @@
 
     cross = (on_chip, partner_col, l)
     diagonal = (r, partner_col, 1 - l)
+    plane_peer = (r, partner_col, l)
     layer_peer = (r, c, 1 - l)
 
     barrier = pltpu.get_barrier_semaphore()
     peers = [(far_row(d), c, l) for d in range(1, n_chip)]
-    peers += [(on_chip, c, l), cross, (r, cw, l), (r, ccw, l), diagonal, layer_peer]
+    peers += [(on_chip, c, l), cross, (r, cw, l), (r, ccw, l), diagonal, plane_peer, layer_peer]
     for peer in peers:
         pl.semaphore_signal(barrier, 1, device_id=peer, device_id_type=MESH)
     pl.semaphore_wait(barrier, len(peers))
@@ -135,29 +136,35 @@
     for d in range(1, n_chip):
         arrival(b_ref.at[0], b_all, b_recv, ((chip + d) % n_chip) * 2 + (1 - core))
 
-    own = jnp.zeros(own_part.shape, jnp.float32)
     far = jnp.zeros(far_part.shape, jnp.float32)
     for s in range(slots):
         for x in range(n_chip):
             jj = s * n_row + 2 * x + half
-            solved = y_all[jj]
-            own = own + multiply(b_all[2 * x + half, s], solved)
-            far = far + multiply(b_all[2 * x + 1 - half, s], solved)
+            far = far + multiply(b_all[2 * x + 1 - half, s], y_all[jj])
+    far_part[...] = far
+    to_diag = pltpu.make_async_remote_copy(
+        far_part, got_diag, p_send.at[0], p_recv.at[0],
+        device_id=diagonal, device_id_type=MESH)
+    to_plane = pltpu.make_async_remote_copy(
+        far_part, got_plane, p_send.at[1], p_recv.at[1],
+        device_id=plane_peer, device_id_type=MESH)
+    to_diag.start()
+    to_plane.start()
+    own = jnp.zeros(own_part.shape, jnp.float32)
+    for s in range(slots):
+        for x in range(n_chip):
+            jj = s * n_row + 2 * x + half
+            own = own + multiply(b_all[2 * x + half, s], y_all[jj])
     own_part[...] = own
-    far_part[...] = far
-
-    first = pltpu.make_async_remote_copy(
-        far_part, got_far, p_send.at[0], p_recv.at[0],
-        device_id=diagonal, device_id_type=MESH)
-    first.start()
-    first.wait()
-    summed[...] = own_part[...] + got_far[...]
-    second = pltpu.make_async_remote_copy(
-        summed, got_sum, p_send.at[1], p_recv.at[1],
+    to_layer = pltpu.make_async_remote_copy(
+        own_part, got_layer, p_send.at[2], p_recv.at[2],
         device_id=layer_peer, device_id_type=MESH)
-    second.start()
-    second.wait()
-    o_ref[...] = a_ref[...] - (summed[...] + got_sum[...])
+    to_layer.start()
+    to_plane.wait()
+    mine = own_part[...] + got_plane[...]
+    to_diag.wait()
+    to_layer.wait()
+    o_ref[...] = a_ref[...] - (mine + (got_layer[...] + got_diag[...]))
 
     for copy in sends + b_sends:
         copy.wait_send()
@@ -187,8 +194,8 @@
             pltpu.SemaphoreType.DMA((n_row,)),
             pltpu.SemaphoreType.DMA((n_col,)),
             pltpu.SemaphoreType.DMA((n_col,)),
-            pltpu.SemaphoreType.DMA((2,)),
-            pltpu.SemaphoreType.DMA((2,)),
+            pltpu.SemaphoreType.DMA((3,)),
+            pltpu.SemaphoreType.DMA((3,)),
         ],
         compiler_params=pltpu.CompilerParams(collective_id=0, has_side_effects=True),
     )(interface_panel, coupling, solved_coupling)

time: 40 us -> 37 us (0.925); the launches traced: 39.4 us -> 36.9 us
  Pallas kernels: 37.9 us -> 35.4 us
    pallas_call x1, Pallas kernels: 37.9 us -> 35.4 us  [shards(): pl.pallas_call(kernel, out_shape=jax.ShapeDtypeStruct((rows, cols), jnp.f...]
where the time goes in v5:
time: 37 us; the launch traced here: 36.9 us
  Pallas kernels  35.4 us (96%)
  local copies, waits for them, and re-layouts  1.47 us (4%)
    pallas_call x1, Pallas kernels, shards(): pl.pallas_call(kernel, out_shape=jax.ShapeDtypeStruct((rows, cols), jnp.f...  35.4 us
    unnamed x1, local copies, waits for them, and re-layouts  1.47 us

profile of v5, /device:TPU:2, one launch (start us, length us, event | category | flops | bytes accessed | tf_op | source)
XLA Modules:
  0.0 36.9 jit_solution(1610670410908909807)
XLA Ops:
  0.0 35.4 %shard_map.37 = f32[128,128]{1,0:T(8,128)} custom-call(f32[128,128]{1,0:T(8,128)} %a_ref.1, f32[1,2,256,128]{3,2,1,0:T(8,128)} %b_ref.1, f32[256,128]{1,0:T(8,128)} %y_ref.1), custom_call_target="tpu_custom_call" | custom-call | tf_op jit(solution)/shard_map/pallas_call | solution.py:184
  35.4 1.5 %copy.5 = f32[128,128]{1,0:T(8,128)} copy(f32[128,128]{1,0:T(8,128)} %shard_map.37) | data formatting | bytes 131072

commit v6 on v5

--- a/solution.py
+++ b/solution.py
@@ -6,6 +6,7 @@
 from jax.sharding import PartitionSpec as P
 
 MESH = pl.DeviceIdType.MESH
+CHUNKS = 4
 
 
 def multiply(block, solved):
@@ -18,7 +19,7 @@
     )
 
 
-def kernel(a_ref, b_ref, y_ref, o_ref, b_all, y_all, own_part, far_part, got_diag, got_plane, got_layer,
+def kernel(b_ref, y_ref, o_ref, b_all, y_all, own_part, far_part, got_diag, got_plane, got_layer,
            b_send, b_recv, y_send, y_recv, p_send, p_recv):
     n_row = lax.axis_size("row")
     n_col = lax.axis_size("col")
@@ -74,22 +75,36 @@
         cross_fill.start()
 
     sends = []
-
-    def y_send_slot(src, slot, col):
+    rows_q = y_ref.shape[0] // CHUNKS
+
+    def piece(q):
+        return pl.ds(q * rows_q, rows_q)
+
+    def y_send_chunk(src, slot, q, col):
         copy = pltpu.make_async_remote_copy(
-            src, y_all.at[slot], y_send.at[len(sends)], y_recv.at[slot],
+            src.at[piece(q)], y_all.at[slot, piece(q)], y_send.at[len(sends)], y_recv.at[slot, q],
             device_id=(r, col, l), device_id_type=MESH)
         copy.start()
         sends.append(copy)
 
-    def y_arrival(slot):
-        arrival(y_ref, y_all, y_recv, slot)
-
-    own_cw, own_ccw = n_z // 2, (n_z - 1) // 2
-    if own_cw >= 1:
-        y_send_slot(y_ref, c, cw)
-    if own_ccw >= 1:
-        y_send_slot(y_ref, c, ccw)
+    def y_arrival(slot, q):
+        pltpu.make_async_remote_copy(
+            y_ref.at[piece(q)], y_all.at[slot, piece(q)], y_recv.at[slot, q], y_recv.at[slot, q],
+            device_id=layer_peer, device_id_type=MESH).wait_recv()
+
+    steps = n_z // 2
+    low, high = list(range(CHUNKS // 2)), list(range(CHUNKS // 2, CHUNKS))
+
+    def cw_chunks(t):
+        return list(range(CHUNKS)) if t < steps else low
+
+    def ccw_chunks(t):
+        return list(range(CHUNKS)) if t < steps else high
+
+    for q in cw_chunks(1):
+        y_send_chunk(y_ref, c, q, cw)
+    for q in ccw_chunks(1):
+        y_send_chunk(y_ref, c, q, ccw)
     y_all[c] = y_ref[...]
 
     @pl.when(keeper)
@@ -113,25 +128,26 @@
         b_send_slot(r, far_row(d))
     b_send_slot(r, on_chip)
 
-    for t in range(2, n_z // 2 + 1):
-        if t <= own_cw:
-            slot = col_of(z - (t - 1), half)
-            y_arrival(slot)
-            y_send_slot(y_all.at[slot], slot, cw)
-        if t <= own_ccw:
-            slot = col_of(z + (t - 1), half)
-            y_arrival(slot)
-            y_send_slot(y_all.at[slot], slot, ccw)
+    for t in range(2, steps + 1):
+        for q in range(CHUNKS):
+            if q in cw_chunks(t - 1):
+                slot = col_of(z - (t - 1), half)
+                y_arrival(slot, q)
+                if q in cw_chunks(t):
+                    y_send_chunk(y_all.at[slot], slot, q, cw)
+            if q in ccw_chunks(t - 1):
+                slot = col_of(z + (t - 1), half)
+                y_arrival(slot, q)
+                if q in ccw_chunks(t):
+                    y_send_chunk(y_all.at[slot], slot, q, ccw)
 
     for d in range(1, n_chip):
         slot = far_row(d)
         arrival(b_ref.at[0], b_all, b_recv, slot)
         b_send_slot(slot, on_chip)
 
-    if own_cw >= 1:
-        y_arrival(col_of(z - own_cw, half))
-    if own_ccw >= 1:
-        y_arrival(col_of(z + own_ccw, half))
+    for q in range(CHUNKS):
+        y_arrival(col_of(z - steps, half), q)
     arrival(b_ref.at[0], b_all, b_recv, on_chip)
     for d in range(1, n_chip):
         arrival(b_ref.at[0], b_all, b_recv, ((chip + d) % n_chip) * 2 + (1 - core))
@@ -164,7 +180,7 @@
     mine = own_part[...] + got_plane[...]
     to_diag.wait()
     to_layer.wait()
-    o_ref[...] = a_ref[...] - (mine + (got_layer[...] + got_diag[...]))
+    o_ref[...] = mine + (got_layer[...] + got_diag[...])
 
     for copy in sends + b_sends:
         copy.wait_send()
@@ -181,10 +197,10 @@
     vmem = pl.BlockSpec(memory_space=pltpu.VMEM)
     rows, cols = interface_panel.shape
     part = pltpu.VMEM((rows, cols), jnp.float32)
-    return pl.pallas_call(
+    summed = pl.pallas_call(
         kernel,
         out_shape=jax.ShapeDtypeStruct((rows, cols), jnp.float32),
-        in_specs=[vmem, vmem, vmem],
+        in_specs=[vmem, vmem],
         out_specs=vmem,
         scratch_shapes=[
             pltpu.VMEM((n_row, slots, depth, width), jnp.float32),
@@ -192,13 +208,14 @@
             part, part, part, part, part,
             pltpu.SemaphoreType.DMA((n_row + 1,)),
             pltpu.SemaphoreType.DMA((n_row,)),
-            pltpu.SemaphoreType.DMA((n_col,)),
-            pltpu.SemaphoreType.DMA((n_col,)),
+            pltpu.SemaphoreType.DMA((n_col * CHUNKS,)),
+            pltpu.SemaphoreType.DMA((n_col, CHUNKS)),
             pltpu.SemaphoreType.DMA((3,)),
             pltpu.SemaphoreType.DMA((3,)),
         ],
         compiler_params=pltpu.CompilerParams(collective_id=0, has_side_effects=True),
-    )(interface_panel, coupling, solved_coupling)
+    )(coupling, solved_coupling)
+    return interface_panel - summed
 
 
 def solution(mesh):

time: 37 us -> 34.5 us (0.932)
  Pallas kernels: 35.4 us -> 32.8 us
  other arithmetic: 0 us -> 1.48 us
  local copies, waits for them, and re-layouts: 1.47 us -> 0.01 us
    pallas_call x1, Pallas kernels: 35.4 us -> 32.8 us  [shards(): pl.pallas_call(kernel, out_shape=jax.ShapeDtypeStruct((rows, cols), jnp.f...]
    sub x0 -> x1, other arithmetic: none -> 1.48 us  [shards(): return interface_panel - summed]
    unnamed x1 -> x2, local copies, waits for them, and re-layouts: 1.47 us -> 0.01 us
where the time goes in v6:
time: 34.5 us; the launch traced here: 34.3 us
  Pallas kernels  32.8 us (95%)
  other arithmetic  1.48 us (4%)
    pallas_call x1, Pallas kernels, shards(): pl.pallas_call(kernel, out_shape=jax.ShapeDtypeStruct((rows, cols), jnp.f...  32.8 us
    sub x1, other arithmetic, shards(): return interface_panel - summed  1.48 us

profile of v6, /device:TPU:2, one launch (start us, length us, event | category | flops | bytes accessed | tf_op | source)
XLA Modules:
  0.0 34.3 jit_solution(3783034310319269469)
XLA Ops:
  0.0 0.0 copy-start
  0.0 32.8 %shard_map.37 = f32[128,128]{1,0:T(8,128)} custom-call(f32[1,2,256,128]{3,2,1,0:T(8,128)} %b_ref.1, f32[256,128]{1,0:T(8,128)} %y_ref.1), custom_call_target="tpu_custom_call" | custom-call | tf_op jit(solution)/shard_map/pallas_call | solution.py:200
  32.8 0.0 copy-done
  32.8 1.5 %sub.3 = f32[128,128]{1,0:T(8,128)} subtract(f32[128,128]{1,0:T(8,128)S(1)} %copy-done, f32[128,128]{1,0:T(8,128)} %shard_map.37) | non-fusion elementwise | flops 16384 | bytes 196608 | tf_op jit(solution)/shard_map/sub | solution.py:218
Async XLA Ops:
  0.0 32.8 %copy-start = (f32[128,128]{1,0:T(8,128)S(1)}, f32[128,128]{1,0:T(8,128)}, u32[]{:S(2)}) copy-start(f32[128,128]{1,0:T(8,128)} %param.3) | copy-start | bytes 196612

commit v7 on v6

--- a/solution.py
+++ b/solution.py
@@ -14,7 +14,7 @@
         block,
         solved,
         (((0,), (0,)), ((), ())),
-        precision=lax.Precision.HIGHEST,
+        precision=lax.Precision.HIGH,
         preferred_element_type=jnp.float32,
     )
 

time: 34.5 us -> 34.1 us (0.988)
  Pallas kernels: 32.8 us -> 32.4 us
    pallas_call x1, Pallas kernels: 32.8 us -> 32.4 us  [shards(): pl.pallas_call(kernel, out_shape=jax.ShapeDtypeStruct((rows, cols), jnp.f...]
where the time goes in v7:
time: 34.1 us; the launch traced here: 33.9 us
  Pallas kernels  32.4 us (95%)
  other arithmetic  1.48 us (4%)
    pallas_call x1, Pallas kernels, shards(): pl.pallas_call(kernel, out_shape=jax.ShapeDtypeStruct((rows, cols), jnp.f...  32.4 us
    sub x1, other arithmetic, shards(): return interface_panel - summed  1.48 us

profile of v7, /device:TPU:2, one launch (start us, length us, event | category | flops | bytes accessed | tf_op | source)
XLA Modules:
  0.0 33.9 jit_solution(13140699711962677982)
XLA Ops:
  0.0 0.0 copy-start
  0.0 32.4 %shard_map.37 = f32[128,128]{1,0:T(8,128)} custom-call(f32[1,2,256,128]{3,2,1,0:T(8,128)} %b_ref.1, f32[256,128]{1,0:T(8,128)} %y_ref.1), custom_call_target="tpu_custom_call" | custom-call | tf_op jit(solution)/shard_map/pallas_call | solution.py:200
  32.4 0.0 copy-done
  32.4 1.5 %sub.3 = f32[128,128]{1,0:T(8,128)} subtract(f32[128,128]{1,0:T(8,128)S(1)} %copy-done, f32[128,128]{1,0:T(8,128)} %shard_map.37) | non-fusion elementwise | flops 16384 | bytes 196608 | tf_op jit(solution)/shard_map/sub | solution.py:218
Async XLA Ops:
  0.0 32.4 %copy-start = (f32[128,128]{1,0:T(8,128)S(1)}, f32[128,128]{1,0:T(8,128)}, u32[]{:S(2)}) copy-start(f32[128,128]{1,0:T(8,128)} %param.3) | copy-start | bytes 196612

commit v8 on v6

--- a/solution.py
+++ b/solution.py
@@ -61,18 +61,26 @@
             src, dst.at[slot], recv_sems.at[slot], recv_sems.at[slot],
             device_id=layer_peer, device_id_type=MESH).wait_recv()
 
-    local_fill = pltpu.make_async_copy(b_ref.at[0], b_all.at[r], b_recv.at[r])
-    cross_fill = pltpu.make_async_remote_copy(
-        b_ref.at[0], b_all.at[on_chip], b_send.at[0], b_recv.at[on_chip],
-        device_id=cross, device_id_type=MESH)
+    rows_b = b_ref.shape[2] // CHUNKS
+
+    def bpiece(q):
+        return pl.ds(q * rows_b, rows_b)
+
+    local_fill = [pltpu.make_async_copy(b_ref.at[0, :, bpiece(q)], b_all.at[r, :, bpiece(q)], b_recv.at[r, q])
+                  for q in range(CHUNKS)]
+    cross_fill = [pltpu.make_async_remote_copy(
+        b_ref.at[0, :, bpiece(q)], b_all.at[on_chip, :, bpiece(q)], b_send.at[q], b_recv.at[on_chip, q],
+        device_id=cross, device_id_type=MESH) for q in range(CHUNKS)]
 
     @pl.when(keeper)
     def _():
-        local_fill.start()
+        for copy in local_fill:
+            copy.start()
 
     @pl.when(jnp.logical_not(keeper))
     def _():
-        cross_fill.start()
+        for copy in cross_fill:
+            copy.start()
 
     sends = []
     rows_q = y_ref.shape[0] // CHUNKS
@@ -92,6 +100,11 @@
             y_ref.at[piece(q)], y_all.at[slot, piece(q)], y_recv.at[slot, q], y_recv.at[slot, q],
             device_id=layer_peer, device_id_type=MESH).wait_recv()
 
+    def b_arrival(slot, q):
+        pltpu.make_async_remote_copy(
+            b_ref.at[0, :, bpiece(q)], b_all.at[slot, :, bpiece(q)], b_recv.at[slot, q], b_recv.at[slot, q],
+            device_id=layer_peer, device_id_type=MESH).wait_recv()
+
     steps = n_z // 2
     low, high = list(range(CHUNKS // 2)), list(range(CHUNKS // 2, CHUNKS))
 
@@ -107,28 +120,36 @@
         y_send_chunk(y_ref, c, q, ccw)
     y_all[c] = y_ref[...]
 
-    @pl.when(keeper)
-    def _():
-        local_fill.wait()
-
-    @pl.when(jnp.logical_not(keeper))
-    def _():
-        arrival(b_ref.at[0], b_all, b_recv, r)
-
     b_sends = []
 
-    def b_send_slot(slot, row):
+    def b_send_chunk(slot, q, row):
         copy = pltpu.make_async_remote_copy(
-            b_all.at[slot], b_all.at[slot], b_send.at[1 + len(b_sends)], b_recv.at[slot],
-            device_id=(row, c, l), device_id_type=MESH)
+            b_all.at[slot, :, bpiece(q)], b_all.at[slot, :, bpiece(q)], b_send.at[CHUNKS + len(b_sends)],
+            b_recv.at[slot, q], device_id=(row, c, l), device_id_type=MESH)
         copy.start()
         b_sends.append(copy)
 
-    for d in range(1, n_chip):
-        b_send_slot(r, far_row(d))
-    b_send_slot(r, on_chip)
-
-    for t in range(2, steps + 1):
+    def b_broadcast():
+        for q in range(CHUNKS):
+            @pl.when(keeper)
+            def _():
+                local_fill[q].wait()
+
+            @pl.when(jnp.logical_not(keeper))
+            def _():
+                b_arrival(r, q)
+
+            for d in range(1, n_chip):
+                b_send_chunk(r, q, far_row(d))
+            b_send_chunk(r, q, on_chip)
+
+    def b_relay():
+        for d in range(1, n_chip):
+            for q in range(CHUNKS):
+                b_arrival(far_row(d), q)
+                b_send_chunk(far_row(d), q, on_chip)
+
+    def y_step(t):
         for q in range(CHUNKS):
             if q in cw_chunks(t - 1):
                 slot = col_of(z - (t - 1), half)
@@ -141,16 +162,21 @@
                 if q in ccw_chunks(t):
                     y_send_chunk(y_all.at[slot], slot, q, ccw)
 
-    for d in range(1, n_chip):
-        slot = far_row(d)
-        arrival(b_ref.at[0], b_all, b_recv, slot)
-        b_send_slot(slot, on_chip)
+    pending = [b_broadcast, b_relay]
+    for t in range(2, steps + 1):
+        y_step(t)
+        if pending:
+            pending.pop(0)()
+    for step in pending:
+        step()
 
     for q in range(CHUNKS):
         y_arrival(col_of(z - steps, half), q)
-    arrival(b_ref.at[0], b_all, b_recv, on_chip)
+    for q in range(CHUNKS):
+        b_arrival(on_chip, q)
     for d in range(1, n_chip):
-        arrival(b_ref.at[0], b_all, b_recv, ((chip + d) % n_chip) * 2 + (1 - core))
+        for q in range(CHUNKS):
+            b_arrival(((chip + d) % n_chip) * 2 + (1 - core), q)
 
     far = jnp.zeros(far_part.shape, jnp.float32)
     for s in range(slots):
@@ -187,7 +213,8 @@
 
     @pl.when(jnp.logical_not(keeper))
     def _():
-        cross_fill.wait_send()
+        for copy in cross_fill:
+            copy.wait_send()
 
 
 def shards(interface_panel, coupling, solved_coupling):
@@ -206,8 +233,8 @@
             pltpu.VMEM((n_row, slots, depth, width), jnp.float32),
             pltpu.VMEM((n_col,) + solved_coupling.shape, jnp.float32),
             part, part, part, part, part,
-            pltpu.SemaphoreType.DMA((n_row + 1,)),
-            pltpu.SemaphoreType.DMA((n_row,)),
+            pltpu.SemaphoreType.DMA((2 * n_row * CHUNKS,)),
+            pltpu.SemaphoreType.DMA((n_row, CHUNKS)),
             pltpu.SemaphoreType.DMA((n_col * CHUNKS,)),
             pltpu.SemaphoreType.DMA((n_col, CHUNKS)),
             pltpu.SemaphoreType.DMA((3,)),

time: 34.5 us -> 40.8 us (1.18)
  the two profiles are of different devices: /device:TPU:2 before, /device:TPU:8 now
where the time goes in v8:
time: 40.8 us; the launch traced here: 40.7 us
  Pallas kernels  39.2 us (96%)
  other arithmetic  1.48 us (4%)
    pallas_call x1, Pallas kernels, shards(): pl.pallas_call(kernel, out_shape=jax.ShapeDtypeStruct((rows, cols), jnp.f...  39.2 us
    sub x1, other arithmetic, shards(): return interface_panel - summed  1.48 us

profile of v8, /device:TPU:8, one launch (start us, length us, event | category | flops | bytes accessed | tf_op | source)
XLA Modules:
  0.0 40.7 jit_solution(3036254226706853030)
XLA Ops:
  0.0 0.0 copy-start
  0.0 39.2 %shard_map.37 = f32[128,128]{1,0:T(8,128)} custom-call(f32[1,2,256,128]{3,2,1,0:T(8,128)} %b_ref.1, f32[256,128]{1,0:T(8,128)} %y_ref.1), custom_call_target="tpu_custom_call" | custom-call | tf_op jit(solution)/shard_map/pallas_call | solution.py:227
  39.2 0.0 copy-done
  39.2 1.5 %sub.3 = f32[128,128]{1,0:T(8,128)} subtract(f32[128,128]{1,0:T(8,128)S(1)} %copy-done, f32[128,128]{1,0:T(8,128)} %shard_map.37) | non-fusion elementwise | flops 16384 | bytes 196608 | tf_op jit(solution)/shard_map/sub | solution.py:245
Async XLA Ops:
  0.0 39.2 %copy-start = (f32[128,128]{1,0:T(8,128)S(1)}, f32[128,128]{1,0:T(8,128)}, u32[]{:S(2)}) copy-start(f32[128,128]{1,0:T(8,128)} %param.3) | copy-start | bytes 196612

commit v9 on v6

--- a/solution.py
+++ b/solution.py
@@ -148,16 +148,20 @@
 
     for q in range(CHUNKS):
         y_arrival(col_of(z - steps, half), q)
-    arrival(b_ref.at[0], b_all, b_recv, on_chip)
-    for d in range(1, n_chip):
-        arrival(b_ref.at[0], b_all, b_recv, ((chip + d) % n_chip) * 2 + (1 - core))
-
-    far = jnp.zeros(far_part.shape, jnp.float32)
+    same = jnp.zeros(far_part.shape, jnp.float32)
     for s in range(slots):
         for x in range(n_chip):
             jj = s * n_row + 2 * x + half
-            far = far + multiply(b_all[2 * x + 1 - half, s], y_all[jj])
-    far_part[...] = far
+            same = same + multiply(b_all[2 * x + core, s], y_all[jj])
+    other = jnp.zeros(far_part.shape, jnp.float32)
+    for d in range(n_chip):
+        partner_chip = (chip + d) % n_chip
+        slot = partner_chip * 2 + (1 - core)
+        arrival(b_ref.at[0], b_all, b_recv, slot)
+        for s in range(slots):
+            other = other + multiply(b_all[slot, s], y_all[s * n_row + 2 * partner_chip + half])
+    far_part[...] = jnp.where(keeper, other, same)
+    own_part[...] = jnp.where(keeper, same, other)
     to_diag = pltpu.make_async_remote_copy(
         far_part, got_diag, p_send.at[0], p_recv.at[0],
         device_id=diagonal, device_id_type=MESH)
@@ -166,12 +170,6 @@
         device_id=plane_peer, device_id_type=MESH)
     to_diag.start()
     to_plane.start()
-    own = jnp.zeros(own_part.shape, jnp.float32)
-    for s in range(slots):
-        for x in range(n_chip):
-            jj = s * n_row + 2 * x + half
-            own = own + multiply(b_all[2 * x + half, s], y_all[jj])
-    own_part[...] = own
     to_layer = pltpu.make_async_remote_copy(
         own_part, got_layer, p_send.at[2], p_recv.at[2],
         device_id=layer_peer, device_id_type=MESH)

time: 34.5 us -> 36.1 us (1.046)
  Pallas kernels: 32.8 us -> 34.4 us
    pallas_call x1, Pallas kernels: 32.8 us -> 34.4 us  [shards(): pl.pallas_call(kernel, out_shape=jax.ShapeDtypeStruct((rows, cols), jnp.f...]
where the time goes in v9:
time: 36.1 us; the launch traced here: 35.9 us
  Pallas kernels  34.4 us (95%)
  other arithmetic  1.48 us (4%)
    pallas_call x1, Pallas kernels, shards(): pl.pallas_call(kernel, out_shape=jax.ShapeDtypeStruct((rows, cols), jnp.f...  34.4 us
    sub x1, other arithmetic, shards(): return interface_panel - summed  1.48 us

profile of v9, /device:TPU:2, one launch (start us, length us, event | category | flops | bytes accessed | tf_op | source)
XLA Modules:
  0.0 35.9 jit_solution(8138800721272357577)
XLA Ops:
  0.0 0.0 copy-start
  0.0 34.4 %shard_map.37 = f32[128,128]{1,0:T(8,128)} custom-call(f32[1,2,256,128]{3,2,1,0:T(8,128)} %b_ref.1, f32[256,128]{1,0:T(8,128)} %y_ref.1), custom_call_target="tpu_custom_call" | custom-call | tf_op jit(solution)/shard_map/pallas_call | solution.py:198
  34.5 0.0 copy-done
  34.5 1.5 %sub.3 = f32[128,128]{1,0:T(8,128)} subtract(f32[128,128]{1,0:T(8,128)S(1)} %copy-done, f32[128,128]{1,0:T(8,128)} %shard_map.37) | non-fusion elementwise | flops 16384 | bytes 196608 | tf_op jit(solution)/shard_map/sub | solution.py:216
Async XLA Ops:
  0.0 34.5 %copy-start = (f32[128,128]{1,0:T(8,128)S(1)}, f32[128,128]{1,0:T(8,128)}, u32[]{:S(2)}) copy-start(f32[128,128]{1,0:T(8,128)} %param.3) | copy-start | bytes 196612

commit v10 on v6

--- a/solution.py
+++ b/solution.py
@@ -148,15 +148,16 @@
 
     for q in range(CHUNKS):
         y_arrival(col_of(z - steps, half), q)
-    arrival(b_ref.at[0], b_all, b_recv, on_chip)
-    for d in range(1, n_chip):
-        arrival(b_ref.at[0], b_all, b_recv, ((chip + d) % n_chip) * 2 + (1 - core))
-
     far = jnp.zeros(far_part.shape, jnp.float32)
-    for s in range(slots):
-        for x in range(n_chip):
-            jj = s * n_row + 2 * x + half
-            far = far + multiply(b_all[2 * x + 1 - half, s], y_all[jj])
+    for x in range(n_chip):
+        slot = 2 * x + 1 - half
+
+        @pl.when(keeper)
+        def _():
+            arrival(b_ref.at[0], b_all, b_recv, slot)
+
+        for s in range(slots):
+            far = far + multiply(b_all[slot, s], y_all[s * n_row + 2 * x + half])
     far_part[...] = far
     to_diag = pltpu.make_async_remote_copy(
         far_part, got_diag, p_send.at[0], p_recv.at[0],
@@ -167,10 +168,15 @@
     to_diag.start()
     to_plane.start()
     own = jnp.zeros(own_part.shape, jnp.float32)
-    for s in range(slots):
-        for x in range(n_chip):
-            jj = s * n_row + 2 * x + half
-            own = own + multiply(b_all[2 * x + half, s], y_all[jj])
+    for x in range(n_chip):
+        slot = 2 * x + half
+
+        @pl.when(jnp.logical_not(keeper))
+        def _():
+            arrival(b_ref.at[0], b_all, b_recv, slot)
+
+        for s in range(slots):
+            own = own + multiply(b_all[slot, s], y_all[s * n_row + 2 * x + half])
     own_part[...] = own
     to_layer = pltpu.make_async_remote_copy(
         own_part, got_layer, p_send.at[2], p_recv.at[2],

time: 34.5 us -> 35.7 us (1.035)
  the two profiles are of different devices: /device:TPU:2 before, /device:TPU:1 now
where the time goes in v10:
time: 35.7 us; the launch traced here: 35.6 us
  Pallas kernels  34.1 us (96%)
  other arithmetic  1.48 us (4%)
    pallas_call x1, Pallas kernels, shards(): pl.pallas_call(kernel, out_shape=jax.ShapeDtypeStruct((rows, cols), jnp.f...  34.1 us
    sub x1, other arithmetic, shards(): return interface_panel - summed  1.48 us

profile of v10, /device:TPU:1, one launch (start us, length us, event | category | flops | bytes accessed | tf_op | source)
XLA Modules:
  0.0 35.6 jit_solution(15990328520791095887)
XLA Ops:
  0.0 0.0 copy-start
  0.0 34.1 %shard_map.37 = f32[128,128]{1,0:T(8,128)} custom-call(f32[1,2,256,128]{3,2,1,0:T(8,128)} %b_ref.1, f32[256,128]{1,0:T(8,128)} %y_ref.1), custom_call_target="tpu_custom_call" | custom-call | tf_op jit(solution)/shard_map/pallas_call | solution.py:206
  34.1 0.0 copy-done
  34.1 1.5 %sub.3 = f32[128,128]{1,0:T(8,128)} subtract(f32[128,128]{1,0:T(8,128)S(1)} %copy-done, f32[128,128]{1,0:T(8,128)} %shard_map.37) | non-fusion elementwise | flops 16384 | bytes 196608 | tf_op jit(solution)/shard_map/sub | solution.py:224
Async XLA Ops:
  0.0 34.1 %copy-start = (f32[128,128]{1,0:T(8,128)S(1)}, f32[128,128]{1,0:T(8,128)}, u32[]{:S(2)}) copy-start(f32[128,128]{1,0:T(8,128)} %param.3) | copy-start | bytes 196612
